TPU v7x, 32 devices: a whole 2x2x4 slice. The times are simulated.
32 devices in a mesh: tm: 8 (over y, x, core), space: 4 (over z).
Axes of the slice: x: 2, y: 2, z: 4, core: 2. Of those that a mesh axis runs over, the one named last changes fastest.
Arguments:
- slice_start: float32 [8, 64, 512], P('tm', None, 'space'), may hold values from -6 to 6
- conductance: float32 [64, 512], P(None, 'space'), may hold values from 0.5 to 2
- excitation: float32 [8, 2, 64, 512], P('tm', None, None, 'space'), may hold values from -6 to 6
- self_blocks: float32 [64, 64, 512], P(None, None, 'space')
- coupling: bfloat16 [6, 64, 64, 512], P(None, None, None, 'space'), may hold values from -0.59765625 to 0.59765625
- neighbour_cols: int32 [6, 512], P(None, 'space'), may hold values from 0 to 511, as said below
- mortar: bfloat16 [64, 64, 256], P(None, None, 'space'), may hold values from -0.59765625 to 0.59765625
- inverse_blocks: float32 [64, 64, 512], P(None, None, 'space')
- offsets: int32 [8], P('tm'), may hold values from 0 to 255
Outputs:
- new_start: float32 [8, 64, 512], P('tm', None, 'space')
- correction: float32 [8, 64, 512], P('tm', None, 'space')
Inputs may be any that keep to these rules, and one draw needn't show every extreme that they name: `neighbour_cols`: every neighbour block lies within 32 blocks of its row along the closed azimuthal order (index modulo 512) and is never the row itself; in every draw some rows reach exactly 32 on each side.
All inputs are finite; a program needn't handle non-finite values.
Results may differ from a plain program's by a relative error of at most 0.0031.
Values may be sent and summed in bfloat16 or wider, within the bound.
No kernel may reach another device: no remote copies, remote signals or barrier semaphores. Data moves between devices by JAX's collectives and lax.ppermute only.
A program may use at most 128 MiB of HBM per device.

v0:
```python
import functools

import jax
import jax.numpy as jnp
from jax import lax
from jax.experimental import pallas as pl
from jax.experimental.pallas import tpu as pltpu
from jax.sharding import PartitionSpec as P

REACH = 32
SUBLANES = 8
GROUP = 8
VMEM = pltpu.MemorySpace.VMEM
SMEM = pltpu.MemorySpace.SMEM
MIB = 1 << 20


def pairing(count):
    return (count & (count - 1)) == 0


def partner(position, slot, count):
    if pairing(count):
        return position ^ slot
    return (position + slot) % count


def slot_of(position, device, count):
    if pairing(count):
        return position ^ device
    return lax.rem(position - device + count, count)


def exchange(block, count):
    return [
        lax.ppermute(block, "space", [(i, partner(i, k, count)) for i in range(count)])
        for k in range(1, count)
    ]


def exchange_next(exact, rounded, count, slices):
    def moved(block, slot):
        pairs = [
            (t * count + i, ((t + 1) % slices) * count + partner(i, slot, count))
            for t in range(slices)
            for i in range(count)
        ]
        return lax.ppermute(block, ("tm", "space"), pairs)

    return moved(exact, 0), [moved(rounded, k) for k in range(1, count)]


def call(body, operands, outputs, scratch=(), limit=8, flops=0, in_specs=None):
    return pl.pallas_call(
        body,
        in_specs=in_specs or [pl.BlockSpec(memory_space=VMEM)] * len(operands),
        out_specs=[pl.BlockSpec(memory_space=VMEM)] * len(outputs),
        out_shape=outputs,
        scratch_shapes=list(scratch),
        compiler_params=pltpu.CompilerParams(vmem_limit_bytes=limit * MIB),
        cost_estimate=pl.CostEstimate(flops=flops, bytes_accessed=MIB, transcendentals=0),
    )(*operands)


def lanes(shape):
    return lax.broadcasted_iota(jnp.int32, shape, len(shape) - 1)


def outer_lanes(shape):
    lane = lanes(shape)
    return (lane < REACH) | (lane >= shape[-1] - REACH)


def round_kernel(start_ref, rounded_ref):
    rounded_ref[...] = start_ref[0].astype(jnp.bfloat16)


def pack_kernel(coupling_ref, mortar_ref, packed_ref, face_ref):
    near, edges, _, blocks = coupling_ref.shape
    half, air = near // 2, mortar_ref.shape[2]
    outer = outer_lanes((edges, blocks))

    def row(i, carry):
        for k in range(half):
            one = coupling_ref[k, i].astype(jnp.float32)
            other = coupling_ref[k + half, i].astype(jnp.float32)
            packed_ref[i, k] = jnp.where(outer, one, pltpu.roll(other, blocks // 2, 1))
        face = mortar_ref[i].astype(jnp.float32)
        face_ref[i] = jnp.concatenate([face[: edges // 2], face[edges // 2 :]], axis=1)
        return carry

    lax.fori_loop(0, edges, row, 0)


def pack(coupling, mortar):
    near, edges, _, blocks = coupling.shape
    operands = [pltpu.with_memory_space_constraint(a, VMEM) for a in (coupling, mortar)]
    outputs = [
        pltpu.VMEM((edges, near // 2, edges, blocks), jnp.float32),
        pltpu.VMEM((edges, edges // 2, blocks), jnp.float32),
    ]
    return call(pack_kernel, operands, outputs, limit=2)


def rounded_wide(x):
    return x.astype(jnp.bfloat16).astype(jnp.float32)


def rows_of(g):
    return pl.ds(pl.multiple_of(g * GROUP, GROUP), GROUP)


def product(matrix, vector):
    depth, blocks = vector.shape
    tiles = depth // SUBLANES
    split = matrix.astype(jnp.float32).reshape(GROUP, tiles, SUBLANES, blocks)
    return jnp.sum(split * vector.reshape(1, tiles, SUBLANES, blocks), axis=1)


def column_places(cols_ref, k, shape, position):
    column = jnp.broadcast_to(cols_ref[k : k + 1, :], shape)
    place = column & (shape[1] - 1)
    return place, column - place == position * shape[1]


def local_body(stage, step, *refs):
    cols_ref, coupling_ref, self_ref, cond_ref, source_ref = refs[:5]
    near_ref, sums_ref = refs[-2:]
    refs = refs[5:-2]
    edges, blocks = cond_ref.shape
    near = cols_ref.shape[0]
    conductance = cond_ref[...]
    if stage in ("third", "fourth"):
        new, old = refs[0][...], refs[1][0]
        source = 0.5 * (source_ref[0, 0] + source_ref[0, 1])
        half = 0.5 * conductance
        rhs = (half * new + source) - (half * old + source)
        scale = 0.5
        if stage == "third":
            x = new - old
            own = rounded_wide(new) - rounded_wide(old)
            part_ref = refs[2]
        else:
            x = refs[2][...]
            own = rounded_wide(x)
            part_ref, arrived_ref = refs[3:]
            arrived_ref[0] = new
    else:
        source = source_ref[0, step]
        base = refs[0][...]
        base = base[0] if base.ndim == 3 else base
        x = base if stage == "first" else refs[1][...]
        rhs = conductance * base + source
        scale = 1.0
        own = rounded_wide(x)
        part_ref = refs[-1]

    position = lax.axis_index("space")
    near_ref[near] = x
    for k in range(near):
        place, inside = column_places(cols_ref, k, (edges, blocks), position)
        near_ref[k] = jnp.where(inside, jnp.take_along_axis(own, place, axis=1), 0.0)

    def rows(g, carry):
        here = rows_of(g)
        total = product(self_ref[here], near_ref[near])
        for k in range(near):
            total = total + product(coupling_ref[k, here], near_ref[k])
        sums_ref[here, :] = jnp.sum(total, axis=1)
        return carry

    lax.fori_loop(0, edges // GROUP, rows, 0)
    part_ref[...] = rhs - (sums_ref[...] + scale * conductance * x)


def remote_body(stage, count, off_ref, cols_ref, packed_ref, face_ref, inv_ref, part_ref, *refs):
    table_ref, near_ref, layer_ref, sums_ref = refs[-4:]
    refs = refs[:-4]
    edges, blocks = part_ref.shape
    near = cols_ref.shape[0]
    half, air = near // 2, blocks // 2
    messages, refs = refs[:count], refs[count:]
    if stage == "third":
        before, refs = refs[:count], refs[count:]
        new_ref, old_ref, out_ref, rounded_ref = refs
        x = new_ref[...] - old_ref[0]
    else:
        x_ref, out_ref, rounded_ref = refs
        x = x_ref[...]
        x = x[0] if x.ndim == 3 else x
    for k in range(count):
        got = messages[k][...].astype(jnp.float32)
        if stage == "third":
            got = got - before[k][...].astype(jnp.float32)
        table_ref[k] = got

    position = lax.axis_index("space")
    after = lax.rem(position + 1, count)
    ahead = lax.rem(position + count - 1, count)
    lane = lanes((edges, blocks))
    outer = outer_lanes((edges, blocks))
    beside = jnp.where(
        lane < air,
        table_ref[slot_of(position, after, count)],
        table_ref[slot_of(position, ahead, count)],
    )

    def reached(k):
        place, inside = column_places(cols_ref, k, (edges, blocks), position)
        return jnp.where(inside, 0.0, jnp.take_along_axis(beside, place, axis=1))

    for k in range(half):
        near_ref[k] = jnp.where(outer, reached(k), pltpu.roll(reached(k + half), blocks // 2, 1))

    turn = off_ref[0]
    low = lax.rem(position + lax.div(turn, air), count)
    high = lax.rem(low + 1, count)
    shift = lax.rem(turn, air)
    layer = jnp.where(
        lane < air,
        table_ref[slot_of(position, low, count)],
        pltpu.roll(table_ref[slot_of(position, high, count)], air, 1),
    )
    facing = pltpu.roll(layer, lax.rem(blocks - shift, blocks), 1)
    deep = edges // 2
    layer_ref[...] = jnp.where(
        lanes((deep, blocks)) < air, facing[:deep], pltpu.roll(facing[deep:], air, 1)
    )

    def rows(g, carry):
        here = rows_of(g)
        total = product(packed_ref[here, 0], near_ref[0])
        for k in range(1, half):
            total = total + product(packed_ref[here, k], near_ref[k])
        far = jnp.sum(total, axis=1)
        face = jnp.sum(product(face_ref[here], layer_ref[...]), axis=1)
        out = outer_lanes(far.shape)
        folded = far + pltpu.roll(far, blocks // 2, 1)
        faced = face + pltpu.roll(face, air, 1)
        sums_ref[here, :] = jnp.where(out, folded, 0.0) + jnp.where(
            lanes(face.shape) < air, faced, 0.0
        )
        return carry

    lax.fori_loop(0, edges // GROUP, rows, 0)
    near_ref[0] = part_ref[...] - sums_ref[...]

    def update(g, carry):
        here = rows_of(g)
        sums_ref[here, :] = jnp.sum(product(inv_ref[here], near_ref[0]), axis=1)
        return carry

    lax.fori_loop(0, edges // GROUP, update, 0)
    result = x + sums_ref[...]
    if stage == "last":
        out_ref[0] = result
    else:
        out_ref[...] = result
        rounded_ref[...] = result.astype(jnp.bfloat16)


def per_device(
    slice_start,
    conductance,
    excitation,
    self_blocks,
    coupling,
    neighbour_cols,
    mortar,
    inverse_blocks,
    offsets,
):
    count = lax.axis_size("space")
    slices = lax.axis_size("tm")
    near, edges, _, blocks = coupling.shape
    field = jax.ShapeDtypeStruct((edges, blocks), jnp.float32)
    short = jax.ShapeDtypeStruct((edges, blocks), jnp.bfloat16)
    whole = jax.ShapeDtypeStruct((1, edges, blocks), jnp.float32)
    keep = functools.partial(pltpu.with_memory_space_constraint, memory_space=VMEM)
    work = 2 * edges * edges * blocks

    (rounded,) = call(round_kernel, [slice_start], [short], flops=1 << 36, limit=1)
    start_near = exchange(rounded, count)
    packed, face = pack(coupling, mortar)

    def local(stage, step, state, outputs=()):
        operands = [neighbour_cols, keep(coupling), keep(self_blocks), conductance, excitation, *state]
        scratch = [
            pltpu.VMEM((near + 1, edges, blocks), jnp.float32),
            pltpu.VMEM((edges, blocks), jnp.float32),
        ]
        body = functools.partial(local_body, stage, step)
        return call(body, operands, [field, *outputs], scratch, flops=work * near)

    def remote(stage, part, messages, state):
        operands = [
            offsets, neighbour_cols, keep(packed), keep(face), keep(inverse_blocks), part,
            *messages, *state,
        ]
        specs = [pl.BlockSpec(memory_space=SMEM)]
        specs += [pl.BlockSpec(memory_space=VMEM)] * (len(operands) - 1)
        scratch = [
            pltpu.VMEM((count, edges, blocks), jnp.float32),
            pltpu.VMEM((near // 2, edges, blocks), jnp.float32),
            pltpu.VMEM((edges // 2, blocks), jnp.float32),
            pltpu.VMEM((edges, blocks), jnp.float32),
        ]
        outputs = [whole] if stage == "last" else [field, short]
        body = functools.partial(remote_body, stage, count)
        if stage == "last":
            body = lambda *refs: remote_body(stage, count, *refs[:-4], None, *refs[-4:])
        return call(body, operands, outputs, scratch, flops=work * near, in_specs=specs)

    start_table = [rounded, *start_near]
    (part,) = local("first", 0, [slice_start])
    x, r = remote("plain", part, start_table, [slice_start])
    got = exchange(r, count)
    (part,) = local("second", 0, [slice_start, x])
    midway, r = remote("plain", part, [r, *got], [x])
    got = exchange(r, count)
    (part,) = local("first", 1, [midway])
    x, r = remote("plain", part, [r, *got], [midway])
    got = exchange(r, count)
    (part,) = local("second", 1, [midway, x])
    fine, r = remote("plain", part, [r, *got], [x])

    arrived, got = exchange_next(fine, r, count, slices)
    (part,) = local("third", 0, [arrived, slice_start])
    arrived_short = arrived.astype(jnp.bfloat16)
    x, r = remote(
        "third", part, [arrived_short, *got], [*start_table, arrived, slice_start]
    )
    got = exchange(r, count)
    part, new_start = local("fourth", 0, [arrived, slice_start, x], [whole])
    (correction,) = remote("last", part, [r, *got], [x])
    return (new_start, correction)


def solution(mesh):
    in_specs = (
        P("tm", None, "space"),
        P(None, "space"),
        P("tm", None, None, "space"),
        P(None, None, "space"),
        P(None, None, None, "space"),
        P(None, "space"),
        P(None, None, "space"),
        P(None, None, "space"),
        P("tm"),
    )
    out_specs = (P("tm", None, "space"), P("tm", None, "space"))
    return jax.shard_map(
        per_device, mesh=mesh, in_specs=in_specs, out_specs=out_specs, check_vma=False
    )
```

profile of v0, /device:TPU:0, one launch (start us, length us, event | category | flops | bytes accessed | tf_op | source)
XLA Modules:
  0.0 65.5 jit_solution(8568232725928035745)
XLA Ops:
  1.6 5.1 %collective-permute-start.2 = (bf16[64,128]{1,0:T(8,128)(2,1)S(1)}, bf16[64,128]{1,0:T(8,128)(2,1)S(1)}, u32[]{:S(2)}, u32[]{:S(2)}) collective-permute-start(bf16[64,128]{1,0:T(8,128)(2,1)S(1)} %shard_map.106.refs_0_.refs_4_), channel_id=1, source_target_pairs={{0,3},{1,2},{2,1},{3,0},{4,7},{5,6},{6,5},{7,4},{8,11},{9,10},{10,... | collective-permute-start | bytes 49160 | tf_op jit(solution)/shard_map/ppermute | solution.py:36
  8.1 5.5 %shard_map.104 = (f32[64,3,64,128]{3,2,1,0:T(8,128)S(1)}, f32[64,32,128]{2,1,0:T(8,128)S(1)}) custom-call(bf16[6,64,64,128]{3,2,1,0:T(8,128)(2,1)S(1)} %copy-done, bf16[64,64,64]{2,1,0:T(8,128)(2,1)S(1)} %copy-done.7), custom_call_target="tpu_custom_call" | custom-call | bytes 1048576 | tf_op jit(solution)/shard_map/pallas_call | solution.py:54
  13.6 1.8 %shard_map.105.part_ref = f32[64,128]{1,0:T(8,128)S(1)} custom-call(s32[6,128]{1,0:T(8,128)S(1)} %copy-done.8, bf16[6,64,64,128]{3,2,1,0:T(8,128)(2,1)S(1)} %copy-done, f32[64,64,128]{2,1,0:T(8,128)S(1)} %copy-done.1, f32[64,128]{1,0:T(8,128)S(1)} %copy-done.4, f32[1,2,64,128]{3,2,1,0:T(8,128)S(1)} %copy-done.3, f32[1,64,128]{2,1,0:T(8,128)S(1)} %copy-done.6), custom_call_target="tpu_custom_call" | custom-call | flops 6291456 | bytes 1048576 | tf_op jit(solution)/shard_map/pallas_call | solution.py:54
  15.5 1.9 %shard_map.107 = (f32[64,128]{1,0:T(8,128)S(1)}, bf16[64,128]{1,0:T(8,128)(2,1)S(1)}) custom-call(s32[1]{0:T(128)S(6)} %copy.11.off_ref.refs_0_, s32[6,128]{1,0:T(8,128)S(1)} %copy-done.8, f32[64,3,64,128]{3,2,1,0:T(8,128)S(1)} %get-tuple-element.16.packed_ref.refs_2_, f32[64,32,128]{2,1,0:T(8,128)S(1)} %get-tuple-element.17.face_ref.refs_3_, ...), custom_call_target="tpu_custom_call" | custom-call | flops 6291456 | bytes 1048576 | tf_op jit(solution)/shard_map/pallas_call | solution.py:54
  17.5 3.8 %collective-permute-start.5 = (bf16[64,128]{1,0:T(8,128)(2,1)S(1)}, bf16[64,128]{1,0:T(8,128)(2,1)S(1)}, u32[]{:S(2)}, u32[]{:S(2)}) collective-permute-start(bf16[64,128]{1,0:T(8,128)(2,1)S(1)} %get-tuple-element.19.refs_0_), channel_id=1, source_target_pairs={{0,3},{1,2},{2,1},{3,0},{4,7},{5,6},{6,5},{7,4},{8,11},{9,10},{10,... | collective-permute-start | bytes 49160 | tf_op jit(solution)/shard_map/ppermute | solution.py:36
  21.9 1.9 %shard_map.108.part_ref = f32[64,128]{1,0:T(8,128)S(1)} custom-call(s32[6,128]{1,0:T(8,128)S(1)} %copy-done.8, bf16[6,64,64,128]{3,2,1,0:T(8,128)(2,1)S(1)} %copy-done, f32[64,64,128]{2,1,0:T(8,128)S(1)} %copy-done.1, f32[64,128]{1,0:T(8,128)S(1)} %copy-done.4, f32[1,2,64,128]{3,2,1,0:T(8,128)S(1)} %copy-done.3, f32[1,64,128]{2,1,0:T(8,128)S(1)} %copy-done.6, ...), custom_call_target="tpu_custom_call" | custom-call | flops 6291456 | bytes 1048576 | tf_op jit(solution)/shard_map/pallas_call | solution.py:54
  23.8 2.1 %collective-permute-done.4.refs_2_ = bf16[64,128]{1,0:T(8,128)(2,1)S(1)} collective-permute-done((bf16[64,128]{1,0:T(8,128)(2,1)S(1)}, bf16[64,128]{1,0:T(8,128)(2,1)S(1)}, u32[]{:S(2)}, u32[]{:S(2)}) %collective-permute-start.4) | collective-permute-done | bytes 16416 | tf_op jit(solution)/shard_map/ppermute | solution.py:36
  25.9 1.9 %shard_map.109 = (f32[64,128]{1,0:T(8,128)S(1)}, bf16[64,128]{1,0:T(8,128)(2,1)S(1)}) custom-call(s32[1]{0:T(128)S(6)} %copy.11.off_ref.refs_0_, s32[6,128]{1,0:T(8,128)S(1)} %copy-done.8, f32[64,3,64,128]{3,2,1,0:T(8,128)S(1)} %get-tuple-element.16.packed_ref.refs_2_, f32[64,32,128]{2,1,0:T(8,128)S(1)} %get-tuple-element.17.face_ref.refs_3_, ...), custom_call_target="tpu_custom_call" | custom-call | flops 6291456 | bytes 1048576 | tf_op jit(solution)/shard_map/pallas_call | solution.py:54
  27.8 1.7 %collective-permute-start.8 = (bf16[64,128]{1,0:T(8,128)(2,1)S(1)}, bf16[64,128]{1,0:T(8,128)(2,1)S(1)}, u32[]{:S(2)}, u32[]{:S(2)}) collective-permute-start(bf16[64,128]{1,0:T(8,128)(2,1)S(1)} %get-tuple-element.21.refs_0_), channel_id=1, source_target_pairs={{0,3},{1,2},{2,1},{3,0},{4,7},{5,6},{6,5},{7,4},{8,11},{9,10},{10,... | collective-permute-start | bytes 49160 | tf_op jit(solution)/shard_map/ppermute | solution.py:36
  30.0 2.3 %collective-permute-start.6 = (bf16[64,128]{1,0:T(8,128)(2,1)S(1)}, bf16[64,128]{1,0:T(8,128)(2,1)S(1)}, u32[]{:S(2)}, u32[]{:S(2)}) collective-permute-start(bf16[64,128]{1,0:T(8,128)(2,1)S(1)} %get-tuple-element.21.refs_0_), channel_id=1, source_target_pairs={{0,1},{1,0},{2,3},{3,2},{4,5},{5,4},{6,7},{7,6},{8,9},{9,8},{10,11... | collective-permute-start | bytes 49160 | tf_op jit(solution)/shard_map/ppermute | solution.py:36
  32.3 1.8 %shard_map.110.part_ref = f32[64,128]{1,0:T(8,128)S(1)} custom-call(s32[6,128]{1,0:T(8,128)S(1)} %copy-done.8, bf16[6,64,64,128]{3,2,1,0:T(8,128)(2,1)S(1)} %copy-done, f32[64,64,128]{2,1,0:T(8,128)S(1)} %copy-done.1, f32[64,128]{1,0:T(8,128)S(1)} %copy-done.4, f32[1,2,64,128]{3,2,1,0:T(8,128)S(1)} %copy-done.3, f32[64,128]{1,0:T(8,128)S(1)} %get-tuple-element.20.refs_5_.refs_4_), custom_call_target="tpu_custom_call" | custom-call | flops 6291456 | bytes 1048576 | tf_op jit(solution)/shard_map/pallas_call | solution.py:54
  34.2 1.9 %shard_map.111 = (f32[64,128]{1,0:T(8,128)S(1)}, bf16[64,128]{1,0:T(8,128)(2,1)S(1)}) custom-call(s32[1]{0:T(128)S(6)} %copy.11.off_ref.refs_0_, s32[6,128]{1,0:T(8,128)S(1)} %copy-done.8, f32[64,3,64,128]{3,2,1,0:T(8,128)S(1)} %get-tuple-element.16.packed_ref.refs_2_, f32[64,32,128]{2,1,0:T(8,128)S(1)} %get-tuple-element.17.face_ref.refs_3_, ...), custom_call_target="tpu_custom_call" | custom-call | flops 6291456 | bytes 1048576 | tf_op jit(solution)/shard_map/pallas_call | solution.py:54
  36.2 2.4 %collective-permute-start.11 = (bf16[64,128]{1,0:T(8,128)(2,1)S(1)}, bf16[64,128]{1,0:T(8,128)(2,1)S(1)}, u32[]{:S(2)}, u32[]{:S(2)}) collective-permute-start(bf16[64,128]{1,0:T(8,128)(2,1)S(1)} %get-tuple-element.23.refs_0_), channel_id=1, source_target_pairs={{0,3},{1,2},{2,1},{3,0},{4,7},{5,6},{6,5},{7,4},{8,11},{9,10},{10,... | collective-permute-start | bytes 49160 | tf_op jit(solution)/shard_map/ppermute | solution.py:36
  39.5 1.1 %collective-permute-start.9 = (bf16[64,128]{1,0:T(8,128)(2,1)S(1)}, bf16[64,128]{1,0:T(8,128)(2,1)S(1)}, u32[]{:S(2)}, u32[]{:S(2)}) collective-permute-start(bf16[64,128]{1,0:T(8,128)(2,1)S(1)} %get-tuple-element.23.refs_0_), channel_id=1, source_target_pairs={{0,1},{1,0},{2,3},{3,2},{4,5},{5,4},{6,7},{7,6},{8,9},{9,8},{10,11... | collective-permute-start | bytes 49160 | tf_op jit(solution)/shard_map/ppermute | solution.py:36
  40.6 1.9 %shard_map.112.part_ref = f32[64,128]{1,0:T(8,128)S(1)} custom-call(s32[6,128]{1,0:T(8,128)S(1)} %copy-done.8, bf16[6,64,64,128]{3,2,1,0:T(8,128)(2,1)S(1)} %copy-done, f32[64,64,128]{2,1,0:T(8,128)S(1)} %copy-done.1, f32[64,128]{1,0:T(8,128)S(1)} %copy-done.4, f32[1,2,64,128]{3,2,1,0:T(8,128)S(1)} %copy-done.3, ...), custom_call_target="tpu_custom_call" | custom-call | flops 6291456 | bytes 1048576 | tf_op jit(solution)/shard_map/pallas_call | solution.py:54
  43.4 1.9 %shard_map.113 = (f32[64,128]{1,0:T(8,128)S(1)}, bf16[64,128]{1,0:T(8,128)(2,1)S(1)}) custom-call(s32[1]{0:T(128)S(6)} %copy.11.off_ref.refs_0_, s32[6,128]{1,0:T(8,128)S(1)} %copy-done.8, f32[64,3,64,128]{3,2,1,0:T(8,128)S(1)} %get-tuple-element.16.packed_ref.refs_2_, f32[64,32,128]{2,1,0:T(8,128)S(1)} %get-tuple-element.17.face_ref.refs_3_, ...), custom_call_target="tpu_custom_call" | custom-call | flops 6291456 | bytes 1048576 | tf_op jit(solution)/shard_map/pallas_call | solution.py:54
  45.4 2.7 %collective-permute-start.15 = (bf16[64,128]{1,0:T(8,128)(2,1)S(1)}, bf16[64,128]{1,0:T(8,128)(2,1)S(1)}, u32[]{:S(2)}, u32[]{:S(2)}) collective-permute-start(bf16[64,128]{1,0:T(8,128)(2,1)S(1)} %get-tuple-element.25), channel_id=1, source_target_pairs={{0,7},{1,6},{2,5},{3,4},{4,11},{5,10},{6,9},{7,8},{8,15},{9,14},{1... | collective-permute-start | bytes 49160 | tf_op jit(solution)/shard_map/ppermute | solution.py:48
  48.5 3.1 %collective-permute-start.13 = (bf16[64,128]{1,0:T(8,128)(2,1)S(1)}, bf16[64,128]{1,0:T(8,128)(2,1)S(1)}, u32[]{:S(2)}, u32[]{:S(2)}) collective-permute-start(bf16[64,128]{1,0:T(8,128)(2,1)S(1)} %get-tuple-element.25), channel_id=1, source_target_pairs={{0,5},{1,4},{2,7},{3,6},{4,9},{5,8},{6,11},{7,10},{8,13},{9,12},{1... | collective-permute-start | bytes 49160 | tf_op jit(solution)/shard_map/ppermute | solution.py:48
  51.7 2.0 %shard_map.114.part_ref = f32[64,128]{1,0:T(8,128)S(1)} custom-call(s32[6,128]{1,0:T(8,128)S(1)} %copy-done.8, bf16[6,64,64,128]{3,2,1,0:T(8,128)(2,1)S(1)} %copy-done, f32[64,64,128]{2,1,0:T(8,128)S(1)} %copy-done.1, f32[64,128]{1,0:T(8,128)S(1)} %copy-done.4, f32[1,2,64,128]{3,2,1,0:T(8,128)S(1)} %copy-done.3, ...), custom_call_target="tpu_custom_call" | custom-call | flops 6291456 | bytes 1048576 | tf_op jit(solution)/shard_map/pallas_call | solution.py:54
  54.1 2.0 %shard_map.115 = (f32[64,128]{1,0:T(8,128)S(1)}, bf16[64,128]{1,0:T(8,128)(2,1)S(1)}) custom-call(s32[1]{0:T(128)S(6)} %copy.11.off_ref.refs_0_, s32[6,128]{1,0:T(8,128)S(1)} %copy-done.8, f32[64,3,64,128]{3,2,1,0:T(8,128)S(1)} %get-tuple-element.16.packed_ref.refs_2_, f32[64,32,128]{2,1,0:T(8,128)S(1)} %get-tuple-element.17.face_ref.refs_3_, ...), custom_call_target="tpu_custom_call" | custom-call | flops 6291456 | bytes 1048576 | tf_op jit(solution)/shard_map/pallas_call | solution.py:54
  56.1 2.2 %collective-permute-start.18 = (bf16[64,128]{1,0:T(8,128)(2,1)S(1)}, bf16[64,128]{1,0:T(8,128)(2,1)S(1)}, u32[]{:S(2)}, u32[]{:S(2)}) collective-permute-start(bf16[64,128]{1,0:T(8,128)(2,1)S(1)} %get-tuple-element.29.refs_6_), channel_id=1, source_target_pairs={{0,3},{1,2},{2,1},{3,0},{4,7},{5,6},{6,5},{7,4},{8,11},{9,10},{10,... | collective-permute-start | bytes 49160 | tf_op jit(solution)/shard_map/ppermute | solution.py:36
  59.0 1.6 %collective-permute-start.16 = (bf16[64,128]{1,0:T(8,128)(2,1)S(1)}, bf16[64,128]{1,0:T(8,128)(2,1)S(1)}, u32[]{:S(2)}, u32[]{:S(2)}) collective-permute-start(bf16[64,128]{1,0:T(8,128)(2,1)S(1)} %get-tuple-element.29.refs_6_), channel_id=1, source_target_pairs={{0,1},{1,0},{2,3},{3,2},{4,5},{5,4},{6,7},{7,6},{8,9},{9,8},{10,11... | collective-permute-start | bytes 49160 | tf_op jit(solution)/shard_map/ppermute | solution.py:36
  60.6 2.3 %shard_map.116 = (f32[64,128]{1,0:T(8,128)S(1)}, f32[1,64,128]{2,1,0:T(8,128)}) custom-call(s32[6,128]{1,0:T(8,128)S(1)} %copy-done.8, bf16[6,64,64,128]{3,2,1,0:T(8,128)(2,1)S(1)} %copy-done, f32[64,64,128]{2,1,0:T(8,128)S(1)} %copy-done.1, f32[64,128]{1,0:T(8,128)S(1)} %copy-done.4, f32[1,2,64,128]{3,2,1,0:T(8,128)S(1)} %copy-done.3, ...), custom_call_target="tpu_custom_call" | custom-call | flops 6291456 | bytes 1048576 | tf_op jit(solution)/shard_map/pallas_call | solution.py:54
  63.0 2.6 %shard_map.117 = f32[1,64,128]{2,1,0:T(8,128)} custom-call(s32[1]{0:T(128)S(6)} %copy.11.off_ref.refs_0_, s32[6,128]{1,0:T(8,128)S(1)} %copy-done.8, f32[64,3,64,128]{3,2,1,0:T(8,128)S(1)} %get-tuple-element.16.packed_ref.refs_2_, f32[64,32,128]{2,1,0:T(8,128)S(1)} %get-tuple-element.17.face_ref.refs_3_, f32[64,64,128]{2,1,0:T(8,128)S(1)} %copy-done.2, ...), custom_call_target="tpu_custom_call" | custom-call | flops 6291456 | bytes 1048576 | tf_op jit(solution)/shard_map/pallas_call | solution.py:54
  (47 shorter events, 6.3 us)
Async XLA Ops:
  1.6 12.0 %copy-start.1 = (f32[64,64,128]{2,1,0:T(8,128)S(1)}, f32[64,64,128]{2,1,0:T(8,128)}, u32[]{:S(2)}) copy-start(f32[64,64,128]{2,1,0:T(8,128)} %refs_2_.11) | copy-start | bytes 6291460
  1.6 12.0 %copy-start.3 = (f32[1,2,64,128]{3,2,1,0:T(8,128)S(1)}, f32[1,2,64,128]{3,2,1,0:T(8,128)}, u32[]{:S(2)}) copy-start(f32[1,2,64,128]{3,2,1,0:T(8,128)} %refs_4_.14) | copy-start | bytes 196612
  1.6 12.0 %copy-start.4 = (f32[64,128]{1,0:T(8,128)S(1)}, f32[64,128]{1,0:T(8,128)}, u32[]{:S(2)}) copy-start(f32[64,128]{1,0:T(8,128)} %refs_3_.11) | copy-start | bytes 98308
  1.6 12.0 %copy-start.6 = (f32[1,64,128]{2,1,0:T(8,128)S(1)}, f32[1,64,128]{2,1,0:T(8,128)}, u32[]{:S(2)}) copy-start(f32[1,64,128]{2,1,0:T(8,128)} %refs_6_.3) | copy-start | bytes 98308
  1.6 12.0 %copy-start.8 = (s32[6,128]{1,0:T(8,128)S(1)}, s32[6,128]{1,0:T(8,128)}, u32[]{:S(2)}) copy-start(s32[6,128]{1,0:T(8,128)} %refs_1_.13) | copy-start | bytes 9220
  1.6 13.9 %collective-permute-start.2 = (bf16[64,128]{1,0:T(8,128)(2,1)S(1)}, bf16[64,128]{1,0:T(8,128)(2,1)S(1)}, u32[]{:S(2)}, u32[]{:S(2)}) collective-permute-start(bf16[64,128]{1,0:T(8,128)(2,1)S(1)} %shard_map.106.refs_0_.refs_4_), channel_id=1, source_target_pairs={{0,3},{1,2},{2,1},{3,0},{4,7},{5,6},{6,5},{7,4},{8,11},{9,10},{10,... | collective-permute-start | bytes 49160 | tf_op jit(solution)/shard_map/ppermute | solution.py:36
  6.8 8.7 %collective-permute-start.1 = (bf16[64,128]{1,0:T(8,128)(2,1)S(1)}, bf16[64,128]{1,0:T(8,128)(2,1)S(1)}, u32[]{:S(2)}, u32[]{:S(2)}) collective-permute-start(bf16[64,128]{1,0:T(8,128)(2,1)S(1)} %shard_map.106.refs_0_.refs_4_), channel_id=1, source_target_pairs={{0,2},{1,3},{2,0},{3,1},{4,6},{5,7},{6,4},{7,5},{8,10},{9,11},{10,... | collective-permute-start | bytes 49160 | tf_op jit(solution)/shard_map/ppermute | solution.py:36
  6.8 8.7 %collective-permute-start = (bf16[64,128]{1,0:T(8,128)(2,1)S(1)}, bf16[64,128]{1,0:T(8,128)(2,1)S(1)}, u32[]{:S(2)}, u32[]{:S(2)}) collective-permute-start(bf16[64,128]{1,0:T(8,128)(2,1)S(1)} %shard_map.106.refs_0_.refs_4_), channel_id=1, source_target_pairs={{0,1},{1,0},{2,3},{3,2},{4,5},{5,4},{6,7},{7,6},{8,9},{9,8},{10,11... | collective-permute-start | bytes 49160 | tf_op jit(solution)/shard_map/ppermute | solution.py:36
  17.5 6.4 %collective-permute-start.5 = (bf16[64,128]{1,0:T(8,128)(2,1)S(1)}, bf16[64,128]{1,0:T(8,128)(2,1)S(1)}, u32[]{:S(2)}, u32[]{:S(2)}) collective-permute-start(bf16[64,128]{1,0:T(8,128)(2,1)S(1)} %get-tuple-element.19.refs_0_), channel_id=1, source_target_pairs={{0,3},{1,2},{2,1},{3,0},{4,7},{5,6},{6,5},{7,4},{8,11},{9,10},{10,... | collective-permute-start | bytes 49160 | tf_op jit(solution)/shard_map/ppermute | solution.py:36
  21.3 4.6 %collective-permute-start.4 = (bf16[64,128]{1,0:T(8,128)(2,1)S(1)}, bf16[64,128]{1,0:T(8,128)(2,1)S(1)}, u32[]{:S(2)}, u32[]{:S(2)}) collective-permute-start(bf16[64,128]{1,0:T(8,128)(2,1)S(1)} %get-tuple-element.19.refs_0_), channel_id=1, source_target_pairs={{0,2},{1,3},{2,0},{3,1},{4,6},{5,7},{6,4},{7,5},{8,10},{9,11},{10,... | collective-permute-start | bytes 49160 | tf_op jit(solution)/shard_map/ppermute | solution.py:36
  21.3 4.6 %collective-permute-start.3 = (bf16[64,128]{1,0:T(8,128)(2,1)S(1)}, bf16[64,128]{1,0:T(8,128)(2,1)S(1)}, u32[]{:S(2)}, u32[]{:S(2)}) collective-permute-start(bf16[64,128]{1,0:T(8,128)(2,1)S(1)} %get-tuple-element.19.refs_0_), channel_id=1, source_target_pairs={{0,1},{1,0},{2,3},{3,2},{4,5},{5,4},{6,7},{7,6},{8,9},{9,8},{10,11... | collective-permute-start | bytes 49160 | tf_op jit(solution)/shard_map/ppermute | solution.py:36
  27.8 6.3 %collective-permute-start.8 = (bf16[64,128]{1,0:T(8,128)(2,1)S(1)}, bf16[64,128]{1,0:T(8,128)(2,1)S(1)}, u32[]{:S(2)}, u32[]{:S(2)}) collective-permute-start(bf16[64,128]{1,0:T(8,128)(2,1)S(1)} %get-tuple-element.21.refs_0_), channel_id=1, source_target_pairs={{0,3},{1,2},{2,1},{3,0},{4,7},{5,6},{6,5},{7,4},{8,11},{9,10},{10,... | collective-permute-start | bytes 49160 | tf_op jit(solution)/shard_map/ppermute | solution.py:36
  29.6 4.6 %collective-permute-start.7 = (bf16[64,128]{1,0:T(8,128)(2,1)S(1)}, bf16[64,128]{1,0:T(8,128)(2,1)S(1)}, u32[]{:S(2)}, u32[]{:S(2)}) collective-permute-start(bf16[64,128]{1,0:T(8,128)(2,1)S(1)} %get-tuple-element.21.refs_0_), channel_id=1, source_target_pairs={{0,2},{1,3},{2,0},{3,1},{4,6},{5,7},{6,4},{7,5},{8,10},{9,11},{10,... | collective-permute-start | bytes 49160 | tf_op jit(solution)/shard_map/ppermute | solution.py:36
  30.0 4.2 %collective-permute-start.6 = (bf16[64,128]{1,0:T(8,128)(2,1)S(1)}, bf16[64,128]{1,0:T(8,128)(2,1)S(1)}, u32[]{:S(2)}, u32[]{:S(2)}) collective-permute-start(bf16[64,128]{1,0:T(8,128)(2,1)S(1)} %get-tuple-element.21.refs_0_), channel_id=1, source_target_pairs={{0,1},{1,0},{2,3},{3,2},{4,5},{5,4},{6,7},{7,6},{8,9},{9,8},{10,11... | collective-permute-start | bytes 49160 | tf_op jit(solution)/shard_map/ppermute | solution.py:36
  36.2 6.4 %collective-permute-start.11 = (bf16[64,128]{1,0:T(8,128)(2,1)S(1)}, bf16[64,128]{1,0:T(8,128)(2,1)S(1)}, u32[]{:S(2)}, u32[]{:S(2)}) collective-permute-start(bf16[64,128]{1,0:T(8,128)(2,1)S(1)} %get-tuple-element.23.refs_0_), channel_id=1, source_target_pairs={{0,3},{1,2},{2,1},{3,0},{4,7},{5,6},{6,5},{7,4},{8,11},{9,10},{10,... | collective-permute-start | bytes 49160 | tf_op jit(solution)/shard_map/ppermute | solution.py:36
  38.6 4.7 %collective-permute-start.10 = (bf16[64,128]{1,0:T(8,128)(2,1)S(1)}, bf16[64,128]{1,0:T(8,128)(2,1)S(1)}, u32[]{:S(2)}, u32[]{:S(2)}) collective-permute-start(bf16[64,128]{1,0:T(8,128)(2,1)S(1)} %get-tuple-element.23.refs_0_), channel_id=1, source_target_pairs={{0,2},{1,3},{2,0},{3,1},{4,6},{5,7},{6,4},{7,5},{8,10},{9,11},{10,... | collective-permute-start | bytes 49160 | tf_op jit(solution)/shard_map/ppermute | solution.py:36
  39.5 3.9 %collective-permute-start.9 = (bf16[64,128]{1,0:T(8,128)(2,1)S(1)}, bf16[64,128]{1,0:T(8,128)(2,1)S(1)}, u32[]{:S(2)}, u32[]{:S(2)}) collective-permute-start(bf16[64,128]{1,0:T(8,128)(2,1)S(1)} %get-tuple-element.23.refs_0_), channel_id=1, source_target_pairs={{0,1},{1,0},{2,3},{3,2},{4,5},{5,4},{6,7},{7,6},{8,9},{9,8},{10,11... | collective-permute-start | bytes 49160 | tf_op jit(solution)/shard_map/ppermute | solution.py:36
  45.4 6.3 %collective-permute-start.12 = (f32[64,128]{1,0:T(8,128)S(1)}, f32[64,128]{1,0:T(8,128)S(1)}, u32[]{:S(2)}, u32[]{:S(2)}) collective-permute-start(f32[64,128]{1,0:T(8,128)S(1)} %get-tuple-element.24), channel_id=1, source_target_pairs={{0,4},{1,5},{2,6},{3,7},{4,8},{5,9},{6,10},{7,11},{8,12},{9,13},{1... | collective-permute-start | bytes 98312 | tf_op jit(solution)/shard_map/ppermute | solution.py:48
  45.4 8.2 %collective-permute-start.15 = (bf16[64,128]{1,0:T(8,128)(2,1)S(1)}, bf16[64,128]{1,0:T(8,128)(2,1)S(1)}, u32[]{:S(2)}, u32[]{:S(2)}) collective-permute-start(bf16[64,128]{1,0:T(8,128)(2,1)S(1)} %get-tuple-element.25), channel_id=1, source_target_pairs={{0,7},{1,6},{2,5},{3,4},{4,11},{5,10},{6,9},{7,8},{8,15},{9,14},{1... | collective-permute-start | bytes 49160 | tf_op jit(solution)/shard_map/ppermute | solution.py:48
  48.1 6.0 %collective-permute-start.14 = (bf16[64,128]{1,0:T(8,128)(2,1)S(1)}, bf16[64,128]{1,0:T(8,128)(2,1)S(1)}, u32[]{:S(2)}, u32[]{:S(2)}) collective-permute-start(bf16[64,128]{1,0:T(8,128)(2,1)S(1)} %get-tuple-element.25), channel_id=1, source_target_pairs={{0,6},{1,7},{2,4},{3,5},{4,10},{5,11},{6,8},{7,9},{8,14},{9,15},{1... | collective-permute-start | bytes 49160 | tf_op jit(solution)/shard_map/ppermute | solution.py:48
  48.5 5.6 %collective-permute-start.13 = (bf16[64,128]{1,0:T(8,128)(2,1)S(1)}, bf16[64,128]{1,0:T(8,128)(2,1)S(1)}, u32[]{:S(2)}, u32[]{:S(2)}) collective-permute-start(bf16[64,128]{1,0:T(8,128)(2,1)S(1)} %get-tuple-element.25), channel_id=1, source_target_pairs={{0,5},{1,4},{2,7},{3,6},{4,9},{5,8},{6,11},{7,10},{8,13},{9,12},{1... | collective-permute-start | bytes 49160 | tf_op jit(solution)/shard_map/ppermute | solution.py:48
  56.1 6.8 %collective-permute-start.18 = (bf16[64,128]{1,0:T(8,128)(2,1)S(1)}, bf16[64,128]{1,0:T(8,128)(2,1)S(1)}, u32[]{:S(2)}, u32[]{:S(2)}) collective-permute-start(bf16[64,128]{1,0:T(8,128)(2,1)S(1)} %get-tuple-element.29.refs_6_), channel_id=1, source_target_pairs={{0,3},{1,2},{2,1},{3,0},{4,7},{5,6},{6,5},{7,4},{8,11},{9,10},{10,... | collective-permute-start | bytes 49160 | tf_op jit(solution)/shard_map/ppermute | solution.py:36
  58.3 4.6 %collective-permute-start.17 = (bf16[64,128]{1,0:T(8,128)(2,1)S(1)}, bf16[64,128]{1,0:T(8,128)(2,1)S(1)}, u32[]{:S(2)}, u32[]{:S(2)}) collective-permute-start(bf16[64,128]{1,0:T(8,128)(2,1)S(1)} %get-tuple-element.29.refs_6_), channel_id=1, source_target_pairs={{0,2},{1,3},{2,0},{3,1},{4,6},{5,7},{6,4},{7,5},{8,10},{9,11},{10,... | collective-permute-start | bytes 49160 | tf_op jit(solution)/shard_map/ppermute | solution.py:36
  59.0 4.0 %collective-permute-start.16 = (bf16[64,128]{1,0:T(8,128)(2,1)S(1)}, bf16[64,128]{1,0:T(8,128)(2,1)S(1)}, u32[]{:S(2)}, u32[]{:S(2)}) collective-permute-start(bf16[64,128]{1,0:T(8,128)(2,1)S(1)} %get-tuple-element.29.refs_6_), channel_id=1, source_target_pairs={{0,1},{1,0},{2,3},{3,2},{4,5},{5,4},{6,7},{7,6},{8,9},{9,8},{10,11... | collective-permute-start | bytes 49160 | tf_op jit(solution)/shard_map/ppermute | solution.py:36
  (4 other events, 22.3 us)
where the time goes:
time: 65.7 us; the launch traced here: 65.5 us
  starting transfers between devices  29.9 us (46%)
  Pallas kernels  29.5 us (45%)
  waiting for transfers between devices  3.69 us (6%)
  between operations  1.53 us (2%)
  local copies, waits for them, and re-layouts  0.95 us (1%)
    pallas_call x14, Pallas kernels, call(): pl.pallas_call(body, in_specs=in_specs or [pl.BlockSpec(memory_space=VMEM...  29.5 us
    ppermute x15, starting transfers between devices, exchange(): lax.ppermute(block, 'space', [(i, partner(i, k, count)) for i in range(co...  23.6 us
    ppermute x4, starting transfers between devices, moved(): return lax.ppermute(block, ('tm', 'space'), pairs)  6.29 us
    ppermute x15, waiting for transfers between devices, exchange(): lax.ppermute(block, 'space', [(i, partner(i, k, count)) for i in range(co...  3.19 us
  transfers between devices with their start and end apart: 19, of which 6 were waited for; matrix products, arithmetic and copies ran while one was open for 0% of the time, Pallas kernels for 26%

commit v1 on v0

--- a/solution.py
+++ b/solution.py
@@ -9,7 +9,10 @@
 
 REACH = 32
 SUBLANES = 8
-GROUP = 8
+PACK = 8
+LOCAL_GROUP = 16
+REMOTE_GROUP = 16
+UPDATE_GROUP = 32
 VMEM = pltpu.MemorySpace.VMEM
 SMEM = pltpu.MemorySpace.SMEM
 MIB = 1 << 20
@@ -75,52 +78,68 @@
     rounded_ref[...] = start_ref[0].astype(jnp.bfloat16)
 
 
-def pack_kernel(coupling_ref, mortar_ref, packed_ref, face_ref):
+def place_of(cols_ref, k, position, shape):
+    blocks = shape[1]
+    column = jnp.broadcast_to(cols_ref[k : k + 1, :], shape)
+    place = column & (blocks - 1)
+    return place, column - place == position * blocks
+
+
+def pack_kernel(coupling_ref, mortar_ref, cols_ref, packed_ref, face_ref, places_ref):
     near, edges, _, blocks = coupling_ref.shape
-    half, air = near // 2, mortar_ref.shape[2]
+    half, middle = near // 2, blocks // 2
     outer = outer_lanes((edges, blocks))
-
-    def row(i, carry):
-        for k in range(half):
-            one = coupling_ref[k, i].astype(jnp.float32)
-            other = coupling_ref[k + half, i].astype(jnp.float32)
-            packed_ref[i, k] = jnp.where(outer, one, pltpu.roll(other, blocks // 2, 1))
-        face = mortar_ref[i].astype(jnp.float32)
-        face_ref[i] = jnp.concatenate([face[: edges // 2], face[edges // 2 :]], axis=1)
+    position = lax.axis_index("space")
+    thin = (SUBLANES, blocks)
+    for k in range(half):
+        wanted = []
+        for kk in (k, k + half):
+            place, inside = place_of(cols_ref, kk, position, thin)
+            wanted.append(jnp.where(inside, -1, place))
+        places_ref[k] = jnp.where(outer_lanes(thin), wanted[0], pltpu.roll(wanted[1], middle, 1))
+
+    def rows(g, carry):
+        for step in range(PACK):
+            i = g * PACK + step
+            for k in range(half):
+                one = coupling_ref[k, i].astype(jnp.float32)
+                other = coupling_ref[k + half, i].astype(jnp.float32)
+                packed_ref[i, k] = jnp.where(outer, one, pltpu.roll(other, middle, 1))
+            face = mortar_ref[i].astype(jnp.float32)
+            face_ref[i] = jnp.concatenate([face[: edges // 2], face[edges // 2 :]], axis=1)
         return carry
 
-    lax.fori_loop(0, edges, row, 0)
-
-
-def pack(coupling, mortar):
+    lax.fori_loop(0, edges // PACK, rows, 0)
+
+
+def pack(coupling, mortar, cols):
     near, edges, _, blocks = coupling.shape
     operands = [pltpu.with_memory_space_constraint(a, VMEM) for a in (coupling, mortar)]
     outputs = [
         pltpu.VMEM((edges, near // 2, edges, blocks), jnp.float32),
         pltpu.VMEM((edges, edges // 2, blocks), jnp.float32),
+        jax.ShapeDtypeStruct((near // 2, SUBLANES, blocks), jnp.int32),
     ]
-    return call(pack_kernel, operands, outputs, limit=2)
+    return call(pack_kernel, [*operands, cols], outputs, limit=2)
 
 
 def rounded_wide(x):
     return x.astype(jnp.bfloat16).astype(jnp.float32)
-
-
-def rows_of(g):
-    return pl.ds(pl.multiple_of(g * GROUP, GROUP), GROUP)
 
 
 def product(matrix, vector):
     depth, blocks = vector.shape
     tiles = depth // SUBLANES
-    split = matrix.astype(jnp.float32).reshape(GROUP, tiles, SUBLANES, blocks)
+    split = matrix.astype(jnp.float32).reshape(-1, tiles, SUBLANES, blocks)
     return jnp.sum(split * vector.reshape(1, tiles, SUBLANES, blocks), axis=1)
 
 
-def column_places(cols_ref, k, shape, position):
-    column = jnp.broadcast_to(cols_ref[k : k + 1, :], shape)
-    place = column & (shape[1] - 1)
-    return place, column - place == position * shape[1]
+def sweep_rows(edges, group, partial):
+    def step(g, carry):
+        partial(pl.ds(pl.multiple_of(g * group, group), group))
+        return carry
+
+    lax.fori_loop(0, edges // group, step, 0)
 
 
 def local_body(stage, step, *refs):
@@ -154,31 +173,31 @@
         scale = 1.0
         own = rounded_wide(x)
         part_ref = refs[-1]
+    part_ref[...] = rhs - scale * conductance * x
 
     position = lax.axis_index("space")
     near_ref[near] = x
     for k in range(near):
-        place, inside = column_places(cols_ref, k, (edges, blocks), position)
+        place, inside = place_of(cols_ref, k, position, (edges, blocks))
         near_ref[k] = jnp.where(inside, jnp.take_along_axis(own, place, axis=1), 0.0)
 
-    def rows(g, carry):
-        here = rows_of(g)
+    def partial(here):
         total = product(self_ref[here], near_ref[near])
         for k in range(near):
             total = total + product(coupling_ref[k, here], near_ref[k])
-        sums_ref[here, :] = jnp.sum(total, axis=1)
-        return carry
-
-    lax.fori_loop(0, edges // GROUP, rows, 0)
-    part_ref[...] = rhs - (sums_ref[...] + scale * conductance * x)
-
-
-def remote_body(stage, count, off_ref, cols_ref, packed_ref, face_ref, inv_ref, part_ref, *refs):
-    table_ref, near_ref, layer_ref, sums_ref = refs[-4:]
-    refs = refs[:-4]
+        sums_ref[here] = total
+
+    sweep_rows(edges, LOCAL_GROUP, partial)
+    part_ref[...] = part_ref[...] - jnp.sum(sums_ref[...], axis=1)
+
+
+def remote_body(
+    stage, count, off_ref, places_ref, packed_ref, face_ref, inv_ref, part_ref, *refs
+):
+    table_ref, near_ref, layer_ref, sums_ref, faces_ref = refs[-5:]
+    refs = refs[:-5]
     edges, blocks = part_ref.shape
-    near = cols_ref.shape[0]
-    half, air = near // 2, blocks // 2
+    half, air, deep = places_ref.shape[0], blocks // 2, edges // 2
     messages, refs = refs[:count], refs[count:]
     if stage == "third":
         before, refs = refs[:count], refs[count:]
@@ -198,60 +217,47 @@
     after = lax.rem(position + 1, count)
     ahead = lax.rem(position + count - 1, count)
     lane = lanes((edges, blocks))
-    outer = outer_lanes((edges, blocks))
     beside = jnp.where(
         lane < air,
         table_ref[slot_of(position, after, count)],
         table_ref[slot_of(position, ahead, count)],
     )
-
-    def reached(k):
-        place, inside = column_places(cols_ref, k, (edges, blocks), position)
-        return jnp.where(inside, 0.0, jnp.take_along_axis(beside, place, axis=1))
-
     for k in range(half):
-        near_ref[k] = jnp.where(outer, reached(k), pltpu.roll(reached(k + half), blocks // 2, 1))
+        place = jnp.broadcast_to(places_ref[k, 0:1], (edges, blocks))
+        taken = jnp.take_along_axis(beside, jnp.maximum(place, 0), axis=1)
+        near_ref[k] = jnp.where(place >= 0, taken, 0.0)
 
     turn = off_ref[0]
     low = lax.rem(position + lax.div(turn, air), count)
     high = lax.rem(low + 1, count)
-    shift = lax.rem(turn, air)
-    layer = jnp.where(
-        lane < air,
-        table_ref[slot_of(position, low, count)],
-        pltpu.roll(table_ref[slot_of(position, high, count)], air, 1),
-    )
-    facing = pltpu.roll(layer, lax.rem(blocks - shift, blocks), 1)
-    deep = edges // 2
-    layer_ref[...] = jnp.where(
-        lanes((deep, blocks)) < air, facing[:deep], pltpu.roll(facing[deep:], air, 1)
-    )
-
-    def rows(g, carry):
-        here = rows_of(g)
+    reach = (lane & (air - 1)) + lax.rem(turn, air)
+    place = reach & (air - 1)
+    facing = jnp.where(
+        reach < air,
+        jnp.take_along_axis(table_ref[slot_of(position, low, count)], place, axis=1),
+        jnp.take_along_axis(table_ref[slot_of(position, high, count)], place, axis=1),
+    )
+    layer_ref[...] = jnp.where(lane[:deep] < air, facing[:deep], facing[deep:])
+
+    def partial(here):
         total = product(packed_ref[here, 0], near_ref[0])
         for k in range(1, half):
             total = total + product(packed_ref[here, k], near_ref[k])
-        far = jnp.sum(total, axis=1)
-        face = jnp.sum(product(face_ref[here], layer_ref[...]), axis=1)
-        out = outer_lanes(far.shape)
-        folded = far + pltpu.roll(far, blocks // 2, 1)
-        faced = face + pltpu.roll(face, air, 1)
-        sums_ref[here, :] = jnp.where(out, folded, 0.0) + jnp.where(
-            lanes(face.shape) < air, faced, 0.0
-        )
-        return carry
-
-    lax.fori_loop(0, edges // GROUP, rows, 0)
-    near_ref[0] = part_ref[...] - sums_ref[...]
-
-    def update(g, carry):
-        here = rows_of(g)
-        sums_ref[here, :] = jnp.sum(product(inv_ref[here], near_ref[0]), axis=1)
-        return carry
-
-    lax.fori_loop(0, edges // GROUP, update, 0)
-    result = x + sums_ref[...]
+        sums_ref[here] = total
+        faces_ref[here] = product(face_ref[here], layer_ref[...])
+
+    sweep_rows(edges, REMOTE_GROUP, partial)
+    far = jnp.sum(sums_ref[...], axis=1)
+    face = jnp.sum(faces_ref[...], axis=1)
+    far = jnp.where(outer_lanes(far.shape), far + pltpu.roll(far, blocks // 2, 1), 0.0)
+    face = jnp.where(lane < air, face + pltpu.roll(face, air, 1), 0.0)
+    near_ref[0] = part_ref[...] - (far + face)
+
+    def update(here):
+        sums_ref[here] = product(inv_ref[here], near_ref[0])
+
+    sweep_rows(edges, UPDATE_GROUP, update)
+    result = x + jnp.sum(sums_ref[...], axis=1)
     if stage == "last":
         out_ref[0] = result
     else:
@@ -281,20 +287,20 @@
 
     (rounded,) = call(round_kernel, [slice_start], [short], flops=1 << 36, limit=1)
     start_near = exchange(rounded, count)
-    packed, face = pack(coupling, mortar)
+    packed, face, places = pack(coupling, mortar, neighbour_cols)
 
     def local(stage, step, state, outputs=()):
         operands = [neighbour_cols, keep(coupling), keep(self_blocks), conductance, excitation, *state]
         scratch = [
             pltpu.VMEM((near + 1, edges, blocks), jnp.float32),
-            pltpu.VMEM((edges, blocks), jnp.float32),
+            pltpu.VMEM((edges, SUBLANES, blocks), jnp.float32),
         ]
         body = functools.partial(local_body, stage, step)
         return call(body, operands, [field, *outputs], scratch, flops=work * near)
 
     def remote(stage, part, messages, state):
         operands = [
-            offsets, neighbour_cols, keep(packed), keep(face), keep(inverse_blocks), part,
+            offsets, places, keep(packed), keep(face), keep(inverse_blocks), part,
             *messages, *state,
         ]
         specs = [pl.BlockSpec(memory_space=SMEM)]
@@ -303,12 +309,13 @@
             pltpu.VMEM((count, edges, blocks), jnp.float32),
             pltpu.VMEM((near // 2, edges, blocks), jnp.float32),
             pltpu.VMEM((edges // 2, blocks), jnp.float32),
-            pltpu.VMEM((edges, blocks), jnp.float32),
+            pltpu.VMEM((edges, SUBLANES, blocks), jnp.float32),
+            pltpu.VMEM((edges, SUBLANES, blocks), jnp.float32),
         ]
         outputs = [whole] if stage == "last" else [field, short]
         body = functools.partial(remote_body, stage, count)
         if stage == "last":
-            body = lambda *refs: remote_body(stage, count, *refs[:-4], None, *refs[-4:])
+            body = lambda *refs: remote_body(stage, count, *refs[:-5], None, *refs[-5:])
         return call(body, operands, outputs, scratch, flops=work * near, in_specs=specs)
 
     start_table = [rounded, *start_near]

time: 65.7 us -> 57.2 us (0.87)
  Pallas kernels: 29.5 us -> 20 us
  waiting for transfers between devices: 3.69 us -> 4.61 us
    pallas_call x14, Pallas kernels: 29.5 us -> 20 us  [call(): pl.pallas_call(body, in_specs=in_specs or [pl.BlockSpec(memory_space=VMEM...]
    ppermute x15, waiting for transfers between devices: 3.19 us -> 3.99 us  [exchange(): lax.ppermute(block, 'space', [(i, partner(i, k, count)) for i in range(co...]
  transfers between devices with their start and end apart: 19 -> 19, of which waited for: 6 -> 7; matrix products, arithmetic and copies ran while one was open for 0% -> 0% of each run, Pallas kernels for 26% -> 22%
where the time goes in v1:
time: 57.2 us; the launch traced here: 57 us
  starting transfers between devices  29.9 us (52%)
  Pallas kernels  20 us (35%)
  waiting for transfers between devices  4.61 us (8%)
  between operations  1.55 us (3%)
  local copies, waits for them, and re-layouts  0.95 us (2%)
    ppermute x15, starting transfers between devices, exchange(): lax.ppermute(block, 'space', [(i, partner(i, k, count)) for i in range(co...  23.6 us
    pallas_call x14, Pallas kernels, call(): pl.pallas_call(body, in_specs=in_specs or [pl.BlockSpec(memory_space=VMEM...  20 us
    ppermute x4, starting transfers between devices, moved(): return lax.ppermute(block, ('tm', 'space'), pairs)  6.29 us
    ppermute x15, waiting for transfers between devices, exchange(): lax.ppermute(block, 'space', [(i, partner(i, k, count)) for i in range(co...  3.99 us
  transfers between devices with their start and end apart: 19, of which 7 were waited for; matrix products, arithmetic and copies ran while one was open for 0% of the time, Pallas kernels for 22%

profile of v1, /device:TPU:0, one launch (start us, length us, event | category | flops | bytes accessed | tf_op | source)
XLA Modules:
  0.0 57.0 jit_solution(1859074856884872864)
XLA Ops:
  1.6 5.1 %collective-permute-start.2 = (bf16[64,128]{1,0:T(8,128)(2,1)S(1)}, bf16[64,128]{1,0:T(8,128)(2,1)S(1)}, u32[]{:S(2)}, u32[]{:S(2)}) collective-permute-start(bf16[64,128]{1,0:T(8,128)(2,1)S(1)} %shard_map.106.refs_0_.refs_4_), channel_id=1, source_target_pairs={{0,3},{1,2},{2,1},{3,0},{4,7},{5,6},{6,5},{7,4},{8,11},{9,10},{10,... | collective-permute-start | bytes 49160 | tf_op jit(solution)/shard_map/ppermute | solution.py:39
  8.1 1.6 %shard_map.104 = (f32[64,3,64,128]{3,2,1,0:T(8,128)S(1)}, f32[64,32,128]{2,1,0:T(8,128)S(1)}, s32[3,8,128]{2,1,0:T(8,128)S(1)}) custom-call(bf16[6,64,64,128]{3,2,1,0:T(8,128)(2,1)S(1)} %copy-done, bf16[64,64,64]{2,1,0:T(8,128)(2,1)S(1)} %copy-done.7, s32[6,128]{1,0:T(8,128)S(1)} %copy-done.8), custom_call_target="tpu_custom_call" | custom-call | bytes 1048576 | tf_op jit(solution)/shard_map/pallas_call | solution.py:57
  9.7 1.8 %shard_map.105.part_ref = f32[64,128]{1,0:T(8,128)S(1)} custom-call(s32[6,128]{1,0:T(8,128)S(1)} %copy-done.8, bf16[6,64,64,128]{3,2,1,0:T(8,128)(2,1)S(1)} %copy-done, f32[64,64,128]{2,1,0:T(8,128)S(1)} %copy-done.1, f32[64,128]{1,0:T(8,128)S(1)} %copy-done.4, f32[1,2,64,128]{3,2,1,0:T(8,128)S(1)} %copy-done.3, f32[1,64,128]{2,1,0:T(8,128)S(1)} %copy-done.6), custom_call_target="tpu_custom_call" | custom-call | flops 6291456 | bytes 1048576 | tf_op jit(solution)/shard_map/pallas_call | solution.py:57
  11.5 1.2 %shard_map.107 = (f32[64,128]{1,0:T(8,128)S(1)}, bf16[64,128]{1,0:T(8,128)(2,1)S(1)}) custom-call(s32[1]{0:T(128)S(6)} %copy.11.off_ref.refs_0_, s32[3,8,128]{2,1,0:T(8,128)S(1)} %get-tuple-element.17.places_ref.refs_1_, f32[64,3,64,128]{3,2,1,0:T(8,128)S(1)} %get-tuple-element.18.packed_ref.refs_2_, f32[64,32,128]{2,1,0:T(8,128)S(1)} %get-tuple-element.19.face_ref.refs_3_, ...), custom_call_target="tpu_custom_call" | custom-call | flops 6291456 | bytes 1048576 | tf_op jit(solution)/shard_map/pallas_call | solution.py:57
  12.7 3.8 %collective-permute-start.5 = (bf16[64,128]{1,0:T(8,128)(2,1)S(1)}, bf16[64,128]{1,0:T(8,128)(2,1)S(1)}, u32[]{:S(2)}, u32[]{:S(2)}) collective-permute-start(bf16[64,128]{1,0:T(8,128)(2,1)S(1)} %get-tuple-element.21.refs_0_), channel_id=1, source_target_pairs={{0,3},{1,2},{2,1},{3,0},{4,7},{5,6},{6,5},{7,4},{8,11},{9,10},{10,... | collective-permute-start | bytes 49160 | tf_op jit(solution)/shard_map/ppermute | solution.py:39
  17.2 1.8 %shard_map.108.part_ref = f32[64,128]{1,0:T(8,128)S(1)} custom-call(s32[6,128]{1,0:T(8,128)S(1)} %copy-done.8, bf16[6,64,64,128]{3,2,1,0:T(8,128)(2,1)S(1)} %copy-done, f32[64,64,128]{2,1,0:T(8,128)S(1)} %copy-done.1, f32[64,128]{1,0:T(8,128)S(1)} %copy-done.4, f32[1,2,64,128]{3,2,1,0:T(8,128)S(1)} %copy-done.3, f32[1,64,128]{2,1,0:T(8,128)S(1)} %copy-done.6, ...), custom_call_target="tpu_custom_call" | custom-call | flops 6291456 | bytes 1048576 | tf_op jit(solution)/shard_map/pallas_call | solution.py:57
  18.9 2.2 %collective-permute-done.4.refs_2_ = bf16[64,128]{1,0:T(8,128)(2,1)S(1)} collective-permute-done((bf16[64,128]{1,0:T(8,128)(2,1)S(1)}, bf16[64,128]{1,0:T(8,128)(2,1)S(1)}, u32[]{:S(2)}, u32[]{:S(2)}) %collective-permute-start.4) | collective-permute-done | bytes 16416 | tf_op jit(solution)/shard_map/ppermute | solution.py:39
  21.2 1.2 %shard_map.109 = (f32[64,128]{1,0:T(8,128)S(1)}, bf16[64,128]{1,0:T(8,128)(2,1)S(1)}) custom-call(s32[1]{0:T(128)S(6)} %copy.11.off_ref.refs_0_, s32[3,8,128]{2,1,0:T(8,128)S(1)} %get-tuple-element.17.places_ref.refs_1_, f32[64,3,64,128]{3,2,1,0:T(8,128)S(1)} %get-tuple-element.18.packed_ref.refs_2_, f32[64,32,128]{2,1,0:T(8,128)S(1)} %get-tuple-element.19.face_ref.refs_3_, ...), custom_call_target="tpu_custom_call" | custom-call | flops 6291456 | bytes 1048576 | tf_op jit(solution)/shard_map/pallas_call | solution.py:57
  22.3 1.6 %collective-permute-start.8 = (bf16[64,128]{1,0:T(8,128)(2,1)S(1)}, bf16[64,128]{1,0:T(8,128)(2,1)S(1)}, u32[]{:S(2)}, u32[]{:S(2)}) collective-permute-start(bf16[64,128]{1,0:T(8,128)(2,1)S(1)} %get-tuple-element.23.refs_0_), channel_id=1, source_target_pairs={{0,3},{1,2},{2,1},{3,0},{4,7},{5,6},{6,5},{7,4},{8,11},{9,10},{10,... | collective-permute-start | bytes 49160 | tf_op jit(solution)/shard_map/ppermute | solution.py:39
  24.5 2.3 %collective-permute-start.6 = (bf16[64,128]{1,0:T(8,128)(2,1)S(1)}, bf16[64,128]{1,0:T(8,128)(2,1)S(1)}, u32[]{:S(2)}, u32[]{:S(2)}) collective-permute-start(bf16[64,128]{1,0:T(8,128)(2,1)S(1)} %get-tuple-element.23.refs_0_), channel_id=1, source_target_pairs={{0,1},{1,0},{2,3},{3,2},{4,5},{5,4},{6,7},{7,6},{8,9},{9,8},{10,11... | collective-permute-start | bytes 49160 | tf_op jit(solution)/shard_map/ppermute | solution.py:39
  26.8 1.8 %shard_map.110.part_ref = f32[64,128]{1,0:T(8,128)S(1)} custom-call(s32[6,128]{1,0:T(8,128)S(1)} %copy-done.8, bf16[6,64,64,128]{3,2,1,0:T(8,128)(2,1)S(1)} %copy-done, f32[64,64,128]{2,1,0:T(8,128)S(1)} %copy-done.1, f32[64,128]{1,0:T(8,128)S(1)} %copy-done.4, f32[1,2,64,128]{3,2,1,0:T(8,128)S(1)} %copy-done.3, f32[64,128]{1,0:T(8,128)S(1)} %get-tuple-element.22.refs_5_.refs_4_), custom_call_target="tpu_custom_call" | custom-call | flops 6291456 | bytes 1048576 | tf_op jit(solution)/shard_map/pallas_call | solution.py:57
  28.7 1.2 %shard_map.111 = (f32[64,128]{1,0:T(8,128)S(1)}, bf16[64,128]{1,0:T(8,128)(2,1)S(1)}) custom-call(s32[1]{0:T(128)S(6)} %copy.11.off_ref.refs_0_, s32[3,8,128]{2,1,0:T(8,128)S(1)} %get-tuple-element.17.places_ref.refs_1_, f32[64,3,64,128]{3,2,1,0:T(8,128)S(1)} %get-tuple-element.18.packed_ref.refs_2_, f32[64,32,128]{2,1,0:T(8,128)S(1)} %get-tuple-element.19.face_ref.refs_3_, ...), custom_call_target="tpu_custom_call" | custom-call | flops 6291456 | bytes 1048576 | tf_op jit(solution)/shard_map/pallas_call | solution.py:57
  29.8 2.5 %collective-permute-start.11 = (bf16[64,128]{1,0:T(8,128)(2,1)S(1)}, bf16[64,128]{1,0:T(8,128)(2,1)S(1)}, u32[]{:S(2)}, u32[]{:S(2)}) collective-permute-start(bf16[64,128]{1,0:T(8,128)(2,1)S(1)} %get-tuple-element.25.refs_0_), channel_id=1, source_target_pairs={{0,3},{1,2},{2,1},{3,0},{4,7},{5,6},{6,5},{7,4},{8,11},{9,10},{10,... | collective-permute-start | bytes 49160 | tf_op jit(solution)/shard_map/ppermute | solution.py:39
  33.2 1.1 %collective-permute-start.9 = (bf16[64,128]{1,0:T(8,128)(2,1)S(1)}, bf16[64,128]{1,0:T(8,128)(2,1)S(1)}, u32[]{:S(2)}, u32[]{:S(2)}) collective-permute-start(bf16[64,128]{1,0:T(8,128)(2,1)S(1)} %get-tuple-element.25.refs_0_), channel_id=1, source_target_pairs={{0,1},{1,0},{2,3},{3,2},{4,5},{5,4},{6,7},{7,6},{8,9},{9,8},{10,11... | collective-permute-start | bytes 49160 | tf_op jit(solution)/shard_map/ppermute | solution.py:39
  34.3 1.8 %shard_map.112.part_ref = f32[64,128]{1,0:T(8,128)S(1)} custom-call(s32[6,128]{1,0:T(8,128)S(1)} %copy-done.8, bf16[6,64,64,128]{3,2,1,0:T(8,128)(2,1)S(1)} %copy-done, f32[64,64,128]{2,1,0:T(8,128)S(1)} %copy-done.1, f32[64,128]{1,0:T(8,128)S(1)} %copy-done.4, f32[1,2,64,128]{3,2,1,0:T(8,128)S(1)} %copy-done.3, ...), custom_call_target="tpu_custom_call" | custom-call | flops 6291456 | bytes 1048576 | tf_op jit(solution)/shard_map/pallas_call | solution.py:57
  37.1 1.2 %shard_map.113 = (f32[64,128]{1,0:T(8,128)S(1)}, bf16[64,128]{1,0:T(8,128)(2,1)S(1)}) custom-call(s32[1]{0:T(128)S(6)} %copy.11.off_ref.refs_0_, s32[3,8,128]{2,1,0:T(8,128)S(1)} %get-tuple-element.17.places_ref.refs_1_, f32[64,3,64,128]{3,2,1,0:T(8,128)S(1)} %get-tuple-element.18.packed_ref.refs_2_, f32[64,32,128]{2,1,0:T(8,128)S(1)} %get-tuple-element.19.face_ref.refs_3_, ...), custom_call_target="tpu_custom_call" | custom-call | flops 6291456 | bytes 1048576 | tf_op jit(solution)/shard_map/pallas_call | solution.py:57
  38.3 2.6 %collective-permute-start.15 = (bf16[64,128]{1,0:T(8,128)(2,1)S(1)}, bf16[64,128]{1,0:T(8,128)(2,1)S(1)}, u32[]{:S(2)}, u32[]{:S(2)}) collective-permute-start(bf16[64,128]{1,0:T(8,128)(2,1)S(1)} %get-tuple-element.27), channel_id=1, source_target_pairs={{0,7},{1,6},{2,5},{3,4},{4,11},{5,10},{6,9},{7,8},{8,15},{9,14},{1... | collective-permute-start | bytes 49160 | tf_op jit(solution)/shard_map/ppermute | solution.py:51
  41.4 3.2 %collective-permute-start.13 = (bf16[64,128]{1,0:T(8,128)(2,1)S(1)}, bf16[64,128]{1,0:T(8,128)(2,1)S(1)}, u32[]{:S(2)}, u32[]{:S(2)}) collective-permute-start(bf16[64,128]{1,0:T(8,128)(2,1)S(1)} %get-tuple-element.27), channel_id=1, source_target_pairs={{0,5},{1,4},{2,7},{3,6},{4,9},{5,8},{6,11},{7,10},{8,13},{9,12},{1... | collective-permute-start | bytes 49160 | tf_op jit(solution)/shard_map/ppermute | solution.py:51
  44.6 1.8 %shard_map.114.part_ref = f32[64,128]{1,0:T(8,128)S(1)} custom-call(s32[6,128]{1,0:T(8,128)S(1)} %copy-done.8, bf16[6,64,64,128]{3,2,1,0:T(8,128)(2,1)S(1)} %copy-done, f32[64,64,128]{2,1,0:T(8,128)S(1)} %copy-done.1, f32[64,128]{1,0:T(8,128)S(1)} %copy-done.4, f32[1,2,64,128]{3,2,1,0:T(8,128)S(1)} %copy-done.3, ...), custom_call_target="tpu_custom_call" | custom-call | flops 6291456 | bytes 1048576 | tf_op jit(solution)/shard_map/pallas_call | solution.py:57
  47.0 1.3 %shard_map.115 = (f32[64,128]{1,0:T(8,128)S(1)}, bf16[64,128]{1,0:T(8,128)(2,1)S(1)}) custom-call(s32[1]{0:T(128)S(6)} %copy.11.off_ref.refs_0_, s32[3,8,128]{2,1,0:T(8,128)S(1)} %get-tuple-element.17.places_ref.refs_1_, f32[64,3,64,128]{3,2,1,0:T(8,128)S(1)} %get-tuple-element.18.packed_ref.refs_2_, f32[64,32,128]{2,1,0:T(8,128)S(1)} %get-tuple-element.19.face_ref.refs_3_, ...), custom_call_target="tpu_custom_call" | custom-call | flops 6291456 | bytes 1048576 | tf_op jit(solution)/shard_map/pallas_call | solution.py:57
  48.3 2.3 %collective-permute-start.18 = (bf16[64,128]{1,0:T(8,128)(2,1)S(1)}, bf16[64,128]{1,0:T(8,128)(2,1)S(1)}, u32[]{:S(2)}, u32[]{:S(2)}) collective-permute-start(bf16[64,128]{1,0:T(8,128)(2,1)S(1)} %get-tuple-element.31.refs_6_), channel_id=1, source_target_pairs={{0,3},{1,2},{2,1},{3,0},{4,7},{5,6},{6,5},{7,4},{8,11},{9,10},{10,... | collective-permute-start | bytes 49160 | tf_op jit(solution)/shard_map/ppermute | solution.py:39
  51.3 1.5 %collective-permute-start.16 = (bf16[64,128]{1,0:T(8,128)(2,1)S(1)}, bf16[64,128]{1,0:T(8,128)(2,1)S(1)}, u32[]{:S(2)}, u32[]{:S(2)}) collective-permute-start(bf16[64,128]{1,0:T(8,128)(2,1)S(1)} %get-tuple-element.31.refs_6_), channel_id=1, source_target_pairs={{0,1},{1,0},{2,3},{3,2},{4,5},{5,4},{6,7},{7,6},{8,9},{9,8},{10,11... | collective-permute-start | bytes 49160 | tf_op jit(solution)/shard_map/ppermute | solution.py:39
  52.8 1.9 %shard_map.116 = (f32[64,128]{1,0:T(8,128)S(1)}, f32[1,64,128]{2,1,0:T(8,128)}) custom-call(s32[6,128]{1,0:T(8,128)S(1)} %copy-done.8, bf16[6,64,64,128]{3,2,1,0:T(8,128)(2,1)S(1)} %copy-done, f32[64,64,128]{2,1,0:T(8,128)S(1)} %copy-done.1, f32[64,128]{1,0:T(8,128)S(1)} %copy-done.4, f32[1,2,64,128]{3,2,1,0:T(8,128)S(1)} %copy-done.3, ...), custom_call_target="tpu_custom_call" | custom-call | flops 6291456 | bytes 1048576 | tf_op jit(solution)/shard_map/pallas_call | solution.py:57
  55.3 1.8 %shard_map.117 = f32[1,64,128]{2,1,0:T(8,128)} custom-call(s32[1]{0:T(128)S(6)} %copy.11.off_ref.refs_0_, s32[3,8,128]{2,1,0:T(8,128)S(1)} %get-tuple-element.17.places_ref.refs_1_, f32[64,3,64,128]{3,2,1,0:T(8,128)S(1)} %get-tuple-element.18.packed_ref.refs_2_, f32[64,32,128]{2,1,0:T(8,128)S(1)} %get-tuple-element.19.face_ref.refs_3_, ...), custom_call_target="tpu_custom_call" | custom-call | flops 6291456 | bytes 1048576 | tf_op jit(solution)/shard_map/pallas_call | solution.py:57
  (47 shorter events, 7.2 us)
Async XLA Ops:
  0.6 7.4 %copy-start = (bf16[6,64,64,128]{3,2,1,0:T(8,128)(2,1)S(1)}, bf16[6,64,64,128]{3,2,1,0:T(8,128)(2,1)}, u32[]{:S(2)}) copy-start(bf16[6,64,64,128]{3,2,1,0:T(8,128)(2,1)} %refs_1_.11) | copy-start | bytes 18874372
  1.6 8.1 %copy-start.1 = (f32[64,64,128]{2,1,0:T(8,128)S(1)}, f32[64,64,128]{2,1,0:T(8,128)}, u32[]{:S(2)}) copy-start(f32[64,64,128]{2,1,0:T(8,128)} %refs_2_.11) | copy-start | bytes 6291460
  1.6 8.1 %copy-start.3 = (f32[1,2,64,128]{3,2,1,0:T(8,128)S(1)}, f32[1,2,64,128]{3,2,1,0:T(8,128)}, u32[]{:S(2)}) copy-start(f32[1,2,64,128]{3,2,1,0:T(8,128)} %refs_4_.14) | copy-start | bytes 196612
  1.6 8.1 %copy-start.4 = (f32[64,128]{1,0:T(8,128)S(1)}, f32[64,128]{1,0:T(8,128)}, u32[]{:S(2)}) copy-start(f32[64,128]{1,0:T(8,128)} %refs_3_.11) | copy-start | bytes 98308
  1.6 8.1 %copy-start.6 = (f32[1,64,128]{2,1,0:T(8,128)S(1)}, f32[1,64,128]{2,1,0:T(8,128)}, u32[]{:S(2)}) copy-start(f32[1,64,128]{2,1,0:T(8,128)} %refs_6_.3) | copy-start | bytes 98308
  1.6 9.9 %collective-permute-start.2 = (bf16[64,128]{1,0:T(8,128)(2,1)S(1)}, bf16[64,128]{1,0:T(8,128)(2,1)S(1)}, u32[]{:S(2)}, u32[]{:S(2)}) collective-permute-start(bf16[64,128]{1,0:T(8,128)(2,1)S(1)} %shard_map.106.refs_0_.refs_4_), channel_id=1, source_target_pairs={{0,3},{1,2},{2,1},{3,0},{4,7},{5,6},{6,5},{7,4},{8,11},{9,10},{10,... | collective-permute-start | bytes 49160 | tf_op jit(solution)/shard_map/ppermute | solution.py:39
  6.8 4.8 %collective-permute-start.1 = (bf16[64,128]{1,0:T(8,128)(2,1)S(1)}, bf16[64,128]{1,0:T(8,128)(2,1)S(1)}, u32[]{:S(2)}, u32[]{:S(2)}) collective-permute-start(bf16[64,128]{1,0:T(8,128)(2,1)S(1)} %shard_map.106.refs_0_.refs_4_), channel_id=1, source_target_pairs={{0,2},{1,3},{2,0},{3,1},{4,6},{5,7},{6,4},{7,5},{8,10},{9,11},{10,... | collective-permute-start | bytes 49160 | tf_op jit(solution)/shard_map/ppermute | solution.py:39
  6.8 4.8 %collective-permute-start = (bf16[64,128]{1,0:T(8,128)(2,1)S(1)}, bf16[64,128]{1,0:T(8,128)(2,1)S(1)}, u32[]{:S(2)}, u32[]{:S(2)}) collective-permute-start(bf16[64,128]{1,0:T(8,128)(2,1)S(1)} %shard_map.106.refs_0_.refs_4_), channel_id=1, source_target_pairs={{0,1},{1,0},{2,3},{3,2},{4,5},{5,4},{6,7},{7,6},{8,9},{9,8},{10,11... | collective-permute-start | bytes 49160 | tf_op jit(solution)/shard_map/ppermute | solution.py:39
  12.7 6.2 %collective-permute-start.5 = (bf16[64,128]{1,0:T(8,128)(2,1)S(1)}, bf16[64,128]{1,0:T(8,128)(2,1)S(1)}, u32[]{:S(2)}, u32[]{:S(2)}) collective-permute-start(bf16[64,128]{1,0:T(8,128)(2,1)S(1)} %get-tuple-element.21.refs_0_), channel_id=1, source_target_pairs={{0,3},{1,2},{2,1},{3,0},{4,7},{5,6},{6,5},{7,4},{8,11},{9,10},{10,... | collective-permute-start | bytes 49160 | tf_op jit(solution)/shard_map/ppermute | solution.py:39
  16.5 4.6 %collective-permute-start.4 = (bf16[64,128]{1,0:T(8,128)(2,1)S(1)}, bf16[64,128]{1,0:T(8,128)(2,1)S(1)}, u32[]{:S(2)}, u32[]{:S(2)}) collective-permute-start(bf16[64,128]{1,0:T(8,128)(2,1)S(1)} %get-tuple-element.21.refs_0_), channel_id=1, source_target_pairs={{0,2},{1,3},{2,0},{3,1},{4,6},{5,7},{6,4},{7,5},{8,10},{9,11},{10,... | collective-permute-start | bytes 49160 | tf_op jit(solution)/shard_map/ppermute | solution.py:39
  16.5 4.6 %collective-permute-start.3 = (bf16[64,128]{1,0:T(8,128)(2,1)S(1)}, bf16[64,128]{1,0:T(8,128)(2,1)S(1)}, u32[]{:S(2)}, u32[]{:S(2)}) collective-permute-start(bf16[64,128]{1,0:T(8,128)(2,1)S(1)} %get-tuple-element.21.refs_0_), channel_id=1, source_target_pairs={{0,1},{1,0},{2,3},{3,2},{4,5},{5,4},{6,7},{7,6},{8,9},{9,8},{10,11... | collective-permute-start | bytes 49160 | tf_op jit(solution)/shard_map/ppermute | solution.py:39
  22.3 6.2 %collective-permute-start.8 = (bf16[64,128]{1,0:T(8,128)(2,1)S(1)}, bf16[64,128]{1,0:T(8,128)(2,1)S(1)}, u32[]{:S(2)}, u32[]{:S(2)}) collective-permute-start(bf16[64,128]{1,0:T(8,128)(2,1)S(1)} %get-tuple-element.23.refs_0_), channel_id=1, source_target_pairs={{0,3},{1,2},{2,1},{3,0},{4,7},{5,6},{6,5},{7,4},{8,11},{9,10},{10,... | collective-permute-start | bytes 49160 | tf_op jit(solution)/shard_map/ppermute | solution.py:39
  23.9 4.7 %collective-permute-start.7 = (bf16[64,128]{1,0:T(8,128)(2,1)S(1)}, bf16[64,128]{1,0:T(8,128)(2,1)S(1)}, u32[]{:S(2)}, u32[]{:S(2)}) collective-permute-start(bf16[64,128]{1,0:T(8,128)(2,1)S(1)} %get-tuple-element.23.refs_0_), channel_id=1, source_target_pairs={{0,2},{1,3},{2,0},{3,1},{4,6},{5,7},{6,4},{7,5},{8,10},{9,11},{10,... | collective-permute-start | bytes 49160 | tf_op jit(solution)/shard_map/ppermute | solution.py:39
  24.5 4.2 %collective-permute-start.6 = (bf16[64,128]{1,0:T(8,128)(2,1)S(1)}, bf16[64,128]{1,0:T(8,128)(2,1)S(1)}, u32[]{:S(2)}, u32[]{:S(2)}) collective-permute-start(bf16[64,128]{1,0:T(8,128)(2,1)S(1)} %get-tuple-element.23.refs_0_), channel_id=1, source_target_pairs={{0,1},{1,0},{2,3},{3,2},{4,5},{5,4},{6,7},{7,6},{8,9},{9,8},{10,11... | collective-permute-start | bytes 49160 | tf_op jit(solution)/shard_map/ppermute | solution.py:39
  29.8 6.2 %collective-permute-start.11 = (bf16[64,128]{1,0:T(8,128)(2,1)S(1)}, bf16[64,128]{1,0:T(8,128)(2,1)S(1)}, u32[]{:S(2)}, u32[]{:S(2)}) collective-permute-start(bf16[64,128]{1,0:T(8,128)(2,1)S(1)} %get-tuple-element.25.refs_0_), channel_id=1, source_target_pairs={{0,3},{1,2},{2,1},{3,0},{4,7},{5,6},{6,5},{7,4},{8,11},{9,10},{10,... | collective-permute-start | bytes 49160 | tf_op jit(solution)/shard_map/ppermute | solution.py:39
  32.3 4.7 %collective-permute-start.10 = (bf16[64,128]{1,0:T(8,128)(2,1)S(1)}, bf16[64,128]{1,0:T(8,128)(2,1)S(1)}, u32[]{:S(2)}, u32[]{:S(2)}) collective-permute-start(bf16[64,128]{1,0:T(8,128)(2,1)S(1)} %get-tuple-element.25.refs_0_), channel_id=1, source_target_pairs={{0,2},{1,3},{2,0},{3,1},{4,6},{5,7},{6,4},{7,5},{8,10},{9,11},{10,... | collective-permute-start | bytes 49160 | tf_op jit(solution)/shard_map/ppermute | solution.py:39
  33.2 3.9 %collective-permute-start.9 = (bf16[64,128]{1,0:T(8,128)(2,1)S(1)}, bf16[64,128]{1,0:T(8,128)(2,1)S(1)}, u32[]{:S(2)}, u32[]{:S(2)}) collective-permute-start(bf16[64,128]{1,0:T(8,128)(2,1)S(1)} %get-tuple-element.25.refs_0_), channel_id=1, source_target_pairs={{0,1},{1,0},{2,3},{3,2},{4,5},{5,4},{6,7},{7,6},{8,9},{9,8},{10,11... | collective-permute-start | bytes 49160 | tf_op jit(solution)/shard_map/ppermute | solution.py:39
  38.3 6.3 %collective-permute-start.12 = (f32[64,128]{1,0:T(8,128)S(1)}, f32[64,128]{1,0:T(8,128)S(1)}, u32[]{:S(2)}, u32[]{:S(2)}) collective-permute-start(f32[64,128]{1,0:T(8,128)S(1)} %get-tuple-element.26), channel_id=1, source_target_pairs={{0,4},{1,5},{2,6},{3,7},{4,8},{5,9},{6,10},{7,11},{8,12},{9,13},{1... | collective-permute-start | bytes 98312 | tf_op jit(solution)/shard_map/ppermute | solution.py:51
  38.3 8.0 %collective-permute-start.15 = (bf16[64,128]{1,0:T(8,128)(2,1)S(1)}, bf16[64,128]{1,0:T(8,128)(2,1)S(1)}, u32[]{:S(2)}, u32[]{:S(2)}) collective-permute-start(bf16[64,128]{1,0:T(8,128)(2,1)S(1)} %get-tuple-element.27), channel_id=1, source_target_pairs={{0,7},{1,6},{2,5},{3,4},{4,11},{5,10},{6,9},{7,8},{8,15},{9,14},{1... | collective-permute-start | bytes 49160 | tf_op jit(solution)/shard_map/ppermute | solution.py:51
  40.9 5.9 %collective-permute-start.14 = (bf16[64,128]{1,0:T(8,128)(2,1)S(1)}, bf16[64,128]{1,0:T(8,128)(2,1)S(1)}, u32[]{:S(2)}, u32[]{:S(2)}) collective-permute-start(bf16[64,128]{1,0:T(8,128)(2,1)S(1)} %get-tuple-element.27), channel_id=1, source_target_pairs={{0,6},{1,7},{2,4},{3,5},{4,10},{5,11},{6,8},{7,9},{8,14},{9,15},{1... | collective-permute-start | bytes 49160 | tf_op jit(solution)/shard_map/ppermute | solution.py:51
  41.4 5.6 %collective-permute-start.13 = (bf16[64,128]{1,0:T(8,128)(2,1)S(1)}, bf16[64,128]{1,0:T(8,128)(2,1)S(1)}, u32[]{:S(2)}, u32[]{:S(2)}) collective-permute-start(bf16[64,128]{1,0:T(8,128)(2,1)S(1)} %get-tuple-element.27), channel_id=1, source_target_pairs={{0,5},{1,4},{2,7},{3,6},{4,9},{5,8},{6,11},{7,10},{8,13},{9,12},{1... | collective-permute-start | bytes 49160 | tf_op jit(solution)/shard_map/ppermute | solution.py:51
  48.3 6.4 %collective-permute-start.18 = (bf16[64,128]{1,0:T(8,128)(2,1)S(1)}, bf16[64,128]{1,0:T(8,128)(2,1)S(1)}, u32[]{:S(2)}, u32[]{:S(2)}) collective-permute-start(bf16[64,128]{1,0:T(8,128)(2,1)S(1)} %get-tuple-element.31.refs_6_), channel_id=1, source_target_pairs={{0,3},{1,2},{2,1},{3,0},{4,7},{5,6},{6,5},{7,4},{8,11},{9,10},{10,... | collective-permute-start | bytes 49160 | tf_op jit(solution)/shard_map/ppermute | solution.py:39
  50.6 4.6 %collective-permute-start.17 = (bf16[64,128]{1,0:T(8,128)(2,1)S(1)}, bf16[64,128]{1,0:T(8,128)(2,1)S(1)}, u32[]{:S(2)}, u32[]{:S(2)}) collective-permute-start(bf16[64,128]{1,0:T(8,128)(2,1)S(1)} %get-tuple-element.31.refs_6_), channel_id=1, source_target_pairs={{0,2},{1,3},{2,0},{3,1},{4,6},{5,7},{6,4},{7,5},{8,10},{9,11},{10,... | collective-permute-start | bytes 49160 | tf_op jit(solution)/shard_map/ppermute | solution.py:39
  51.3 4.0 %collective-permute-start.16 = (bf16[64,128]{1,0:T(8,128)(2,1)S(1)}, bf16[64,128]{1,0:T(8,128)(2,1)S(1)}, u32[]{:S(2)}, u32[]{:S(2)}) collective-permute-start(bf16[64,128]{1,0:T(8,128)(2,1)S(1)} %get-tuple-element.31.refs_6_), channel_id=1, source_target_pairs={{0,1},{1,0},{2,3},{3,2},{4,5},{5,4},{6,7},{7,6},{8,9},{9,8},{10,11... | collective-permute-start | bytes 49160 | tf_op jit(solution)/shard_map/ppermute | solution.py:39
  (4 other events, 17.4 us)
